TPU v7x, 32 devices: a whole 2x2x4 slice. The times are simulated.
32 devices in a mesh: dp: 8 (over z, y), row: 2 (over core), col: 2 (over x).
Axes of the slice: x: 2, y: 2, z: 4, core: 2. Of those that a mesh axis runs over, the one named last changes fastest.
Arguments:
- tokens: bfloat16 [32768, 768], P(('dp', 'col'), 'row'), may hold values from -6 to 6
- w_query: float32 [768, 768], P('row', 'col'), may hold values from -0.21875 to 0.21875
- w_key: float32 [768, 768], P('row', 'col'), may hold values from -0.21875 to 0.21875
- w_value: float32 [768, 768], P('row', 'col'), may hold values from -0.21875 to 0.21875
- w_attn_out: float32 [768, 768], P('col', 'row'), may hold values from -0.875 to 0.875
- w_inter: float32 [768, 3072], P('row', 'col'), may hold values from -0.21875 to 0.21875
- w_ffout: float32 [3072, 768], P('col', 'row'), may hold values from -0.109375 to 0.109375
- b_query: float32 [768], replicated, may hold values from -3 to 3
- b_value: float32 [768], replicated, may hold values from -3 to 3
- b_attn_out: float32 [768], replicated, may hold values from -3 to 3
- b_inter: float32 [3072], replicated, may hold values from -3 to 3
- b_ffout: float32 [768], replicated, may hold values from -3 to 3
- gain_one: float32 [768], replicated, may hold values from 0.25 to 1.75
- shift_one: float32 [768], replicated, may hold values from -3 to 3
- gain_two: float32 [768], replicated, may hold values from 0.25 to 1.75
- shift_two: float32 [768], replicated, may hold values from -3 to 3
- lengths: int32 [16], replicated, may hold values from 1025 to 2048, as said below
- block_order: int32 [12, 2], replicated, may hold values from 0 to 1, each once within a row
- cotangent: bfloat16 [32768, 768], P(('dp', 'col'), 'row'), may hold values from -6 to 6
Outputs:
- layer_out: bfloat16 [32768, 768], P(('dp', 'col'), 'row')
- grad_tokens: float32 [32768, 768], P(('dp', 'col'), 'row')
- grad_w_query: float32 [768, 768], P('row', 'col')
- grad_w_key: float32 [768, 768], P('row', 'col')
- grad_w_value: float32 [768, 768], P('row', 'col')
- grad_w_attn_out: float32 [768, 768], P('col', 'row')
- grad_w_inter: float32 [768, 3072], P('row', 'col')
- grad_w_ffout: float32 [3072, 768], P('col', 'row')
- grad_b_query: float32 [768], replicated
- grad_b_value: float32 [768], replicated
- grad_b_attn_out: float32 [768], replicated
- grad_b_inter: float32 [3072], replicated
- grad_b_ffout: float32 [768], replicated
- grad_gain_one: float32 [768], replicated
- grad_shift_one: float32 [768], replicated
- grad_gain_two: float32 [768], replicated
- grad_shift_two: float32 [768], replicated
Inputs may be any that keep to these rules, and one draw needn't show every extreme that they name: `lengths`: every sequence is longer than half of 2048; one sequence fills all 2048 slots. `block_order`: each row holds 0 and 1 once each.
All inputs are finite; a program needn't handle non-finite values.
Results may differ from a plain program's by a relative error of at most 0.02.
Values may be sent and summed in bfloat16 or wider, within the bound.
No kernel may reach another device: no remote copies, remote signals or barrier semaphores. Data moves between devices by JAX's collectives and lax.ppermute only.
A program may use at most 192 MiB of HBM per device.

v0:
```python
import jax
import jax.numpy as jnp
from jax import lax
from jax.sharding import PartitionSpec as P

D = 768
HD = 64
FF = 3072
SEQ = 2048
eps_norm = 1e-05
masked_score = -1e30


def product(left, right):
    return jnp.dot(left, right, preferred_element_type=jnp.float32)


def transposed(left, right):
    return lax.dot_general(
        left, right, (((1,), (1,)), ((), ())), preferred_element_type=jnp.float32
    )


def outer_sum(left, right):
    return lax.dot_general(
        left, right, (((0,), (0,)), ((), ())), preferred_element_type=jnp.float32
    )


def gelu_exact(values):
    return jax.nn.gelu(values, approximate=False)


def placed(values, start, total):
    return lax.dynamic_update_slice(jnp.zeros((total,), jnp.float32), values, (start,))


def gather_cols(values):
    return lax.all_gather(values, "col", axis=0, tiled=True)


def gather_rows(values):
    return lax.all_gather(values, "row", axis=0, tiled=True)


def sum_rows(values):
    return lax.psum_scatter(values, "row", scatter_dimension=0, tiled=True)


def sum_cols(values):
    return lax.psum_scatter(
        values.astype(jnp.bfloat16), "col", scatter_dimension=0, tiled=True
    ).astype(jnp.float32)


def shared_sums(total_one, total_two):
    return lax.psum((total_one, total_two), "row")


def norm_forward(values, gain, shift, reducer):
    total, squares = reducer(jnp.sum(values, 1), jnp.sum(values * values, 1))
    mean = total / D
    variance = squares / D - mean * mean
    scale = lax.rsqrt(variance + eps_norm)
    normal = (values - mean[:, None]) * scale[:, None]
    return (normal * gain + shift, normal, scale)


def norm_backward(grad, normal, scale, gain, reducer):
    inner = grad * gain
    sum_plain, sum_normal = reducer(jnp.sum(inner, 1), jnp.sum(inner * normal, 1))
    return scale[:, None] * (inner - sum_plain[:, None] / D - normal * (sum_normal / D)[:, None])


def head_block(
    query, key_all, value_all, orders, lengths_here, index, heads_local, parts, my_part, seq_rows
):
    half = SEQ // 2
    per_seq = heads_local * parts
    seq_index = index // per_seq
    head = index % per_seq // parts
    offset = index % parts
    part = offset + my_part
    source = orders[head, part]
    query_row = seq_index * seq_rows + offset * half
    select = source * 0
    key_row = seq_index * seq_rows + source * half
    column = head * HD
    query_block = lax.dynamic_slice(query, (query_row, column), (half, HD))
    key_block = lax.dynamic_slice(key_all, (select, key_row, column), (1, half, HD))[0]
    value_block = lax.dynamic_slice(value_all, (select, key_row, column), (1, half, HD))[0]
    positions = source * half + jnp.arange(half)
    live = positions < lengths_here[seq_index]
    scores = transposed(query_block, key_block) * HD ** (-0.5)
    scores = jnp.where(live[None, :], scores, masked_score)
    return (query_row, key_row, select, column, head, query_block, key_block, value_block, scores)


def attend_forward(query, key_all, value_all, orders, lengths_here, parts, my_part, seq_rows):
    rows, width = query.shape
    heads_local = width // HD
    count = rows // seq_rows * heads_local * parts

    def step(index, carry):
        blended_attention_output, logsum = carry
        query_row, key_row, select, column, head, query_block, key_block, value_block, scores = (
            head_block(
                query,
                key_all,
                value_all,
                orders,
                lengths_here,
                index,
                heads_local,
                parts,
                my_part,
                seq_rows,
            )
        )
        top = jnp.max(scores, 1, keepdims=True)
        expo = jnp.exp(scores - top)
        total = jnp.sum(expo, 1, keepdims=True)
        attention_probabilities = (expo / total).astype(jnp.bfloat16)
        blended_attention_output = lax.dynamic_update_slice(
            blended_attention_output,
            product(attention_probabilities, value_block),
            (query_row, column),
        )
        logsum = lax.dynamic_update_slice(logsum, top + jnp.log(total), (query_row, head))
        return (blended_attention_output, logsum)

    start = (jnp.zeros((rows, width), jnp.float32), jnp.zeros((rows, heads_local), jnp.float32))
    return lax.fori_loop(0, count, step, start)


def attend_backward(
    query, key_all, value_all, grad_mixed, logsum, orders, lengths_here, parts, my_part, seq_rows
):
    rows, width = query.shape
    heads_local = width // HD
    count = rows // seq_rows * heads_local * parts
    half = SEQ // 2

    def step(index, carry):
        grad_query, grad_key, grad_value = carry
        query_row, key_row, select, column, head, query_block, key_block, value_block, scores = (
            head_block(
                query,
                key_all,
                value_all,
                orders,
                lengths_here,
                index,
                heads_local,
                parts,
                my_part,
                seq_rows,
            )
        )
        logsum_block = lax.dynamic_slice(logsum, (query_row, head), (half, 1))
        attention_probabilities = jnp.exp(scores - logsum_block)
        grad_block = lax.dynamic_slice(grad_mixed, (query_row, column), (half, HD))
        grad_probs = transposed(grad_block, value_block)
        inner = jnp.sum(grad_probs * attention_probabilities, 1, keepdims=True)
        grad_scores = (attention_probabilities * (grad_probs - inner) * HD ** (-0.5)).astype(
            jnp.bfloat16
        )
        grad_query = lax.dynamic_update_slice(
            grad_query, product(grad_scores, key_block), (query_row, column)
        )
        grad_key = lax.dynamic_update_slice(
            grad_key, outer_sum(grad_scores, query_block)[None], (select, key_row, column)
        )
        grad_value = lax.dynamic_update_slice(
            grad_value,
            outer_sum(attention_probabilities.astype(jnp.bfloat16), grad_block)[None],
            (select, key_row, column),
        )
        return (grad_query, grad_key, grad_value)

    empty_query = jnp.zeros((rows, width), jnp.float32)
    empty_keys = jnp.zeros(key_all.shape, jnp.float32)
    return lax.fori_loop(0, count, step, (empty_query, empty_keys, empty_keys))


def grid_plan(tokens, weights, vectors, lengths, block_order, cotangent):
    w_query, w_key, w_value, w_attn_out, w_inter, w_ffout = weights
    b_query, b_value, b_attn_out, b_inter, b_ffout, gain_one, shift_one, gain_two, shift_two = (
        vectors
    )
    rows_col, width_row = tokens.shape
    width_col = w_query.shape[1]
    ff_col = w_inter.shape[1]
    n_row = lax.axis_size("row")
    n_col = lax.axis_size("col")
    row_index = lax.axis_index("row")
    col_index = lax.axis_index("col")
    group_rows = rows_col * n_col
    rows_row = group_rows // n_row
    per_col = rows_col // SEQ
    per_row = rows_row // SEQ
    group_first = lax.axis_index("dp") * (group_rows // SEQ)
    lengths_col = lax.dynamic_slice(lengths, (group_first + col_index * per_col,), (per_col,))
    lengths_row = lax.dynamic_slice(lengths, (group_first + row_index * per_row,), (per_row,))
    live = (
        (jnp.arange(SEQ)[None, :] < lengths_col[:, None]).astype(jnp.float32).reshape(rows_col, 1)
    )
    heads_local = width_col // HD
    orders = lax.dynamic_slice(block_order, (col_index * heads_local, 0), (heads_local, 2))
    row_start = row_index * width_row
    col_start = col_index * width_col
    ff_start = col_index * ff_col
    b_query_here = lax.dynamic_slice_in_dim(b_query, col_start, width_col)
    b_value_here = lax.dynamic_slice_in_dim(b_value, col_start, width_col)
    b_inter_here = lax.dynamic_slice_in_dim(b_inter, ff_start, ff_col)
    b_attn_here = lax.dynamic_slice_in_dim(b_attn_out, row_start, width_row)
    b_ffout_here = lax.dynamic_slice_in_dim(b_ffout, row_start, width_row)
    gain_one_here = lax.dynamic_slice_in_dim(gain_one, row_start, width_row)
    shift_one_here = lax.dynamic_slice_in_dim(shift_one, row_start, width_row)
    gain_two_here = lax.dynamic_slice_in_dim(gain_two, row_start, width_row)
    shift_two_here = lax.dynamic_slice_in_dim(shift_two, row_start, width_row)
    qkv_w = jnp.concatenate(
        [w_query.astype(jnp.bfloat16), w_key.astype(jnp.bfloat16), w_value.astype(jnp.bfloat16)], 1
    )
    attn_w = w_attn_out.astype(jnp.bfloat16)
    inter_w = w_inter.astype(jnp.bfloat16)
    ffout_w = w_ffout.astype(jnp.bfloat16)
    whole_tokens = gather_cols(tokens)
    qkv_total = sum_rows(product(whole_tokens, qkv_w))
    query_low = (qkv_total[:, :width_col] + b_query_here).astype(jnp.bfloat16)
    key_low = qkv_total[:, width_col : 2 * width_col].astype(jnp.bfloat16)
    value_low = (qkv_total[:, 2 * width_col :] + b_value_here).astype(jnp.bfloat16)
    blended_attention_output, logsum = attend_forward(
        query_low, key_low[None], value_low[None], orders, lengths_row, 2, 0, SEQ
    )
    whole_mixed = gather_rows(blended_attention_output.astype(jnp.bfloat16))
    residual_one = tokens.astype(jnp.float32) + sum_cols(product(whole_mixed, attn_w)) + b_attn_here
    normed_one, normal_one, scale_one = norm_forward(
        residual_one, gain_one_here, shift_one_here, shared_sums
    )
    whole_normed = gather_cols(normed_one.astype(jnp.bfloat16))
    hidden_pre = sum_rows(product(whole_normed, inter_w)) + b_inter_here
    hidden, gelu_back = jax.vjp(gelu_exact, hidden_pre)
    whole_hidden = gather_rows(hidden.astype(jnp.bfloat16))
    residual_two = normed_one + sum_cols(product(whole_hidden, ffout_w)) + b_ffout_here
    layer_out, normal_two, scale_two = norm_forward(
        residual_two, gain_two_here, shift_two_here, shared_sums
    )
    grad_out = cotangent.astype(jnp.float32) * live
    grad_gain_two = jnp.sum(grad_out * normal_two, 0)
    grad_shift_two = jnp.sum(grad_out, 0)
    grad_two = norm_backward(grad_out, normal_two, scale_two, gain_two_here, shared_sums)
    grad_b_ffout = jnp.sum(grad_two, 0)
    whole_grad_two = gather_cols(grad_two.astype(jnp.bfloat16))
    grad_hidden = sum_rows(transposed(whole_grad_two, ffout_w))
    grad_w_ffout = outer_sum(whole_hidden, whole_grad_two)
    (grad_pre,) = gelu_back(grad_hidden)
    grad_pre_low = grad_pre.astype(jnp.bfloat16)
    grad_b_inter = jnp.sum(grad_pre_low.astype(jnp.float32), 0)
    whole_grad_pre = gather_rows(grad_pre_low)
    grad_w_inter = outer_sum(whole_normed, whole_grad_pre)
    grad_normed = grad_two + sum_cols(transposed(whole_grad_pre, inter_w))
    grad_gain_one = jnp.sum(grad_normed * normal_one, 0)
    grad_shift_one = jnp.sum(grad_normed, 0)
    grad_one = norm_backward(grad_normed, normal_one, scale_one, gain_one_here, shared_sums)
    grad_b_attn_out = jnp.sum(grad_one, 0)
    whole_grad_one = gather_cols(grad_one.astype(jnp.bfloat16))
    grad_mixed = sum_rows(transposed(whole_grad_one, attn_w))
    grad_w_attn_out = outer_sum(whole_mixed, whole_grad_one)
    grad_query, grad_key, grad_value = attend_backward(
        query_low,
        key_low[None],
        value_low[None],
        grad_mixed.astype(jnp.bfloat16),
        logsum,
        orders,
        lengths_row,
        2,
        0,
        SEQ,
    )
    grad_qkv_low = jnp.concatenate(
        [
            grad_query.astype(jnp.bfloat16),
            grad_key[0].astype(jnp.bfloat16),
            grad_value[0].astype(jnp.bfloat16),
        ],
        1,
    )
    grad_b_query = jnp.sum(grad_qkv_low[:, :width_col].astype(jnp.float32), 0)
    grad_b_value = jnp.sum(grad_qkv_low[:, 2 * width_col :].astype(jnp.float32), 0)
    whole_grad_qkv = gather_rows(grad_qkv_low)
    grad_tokens = grad_one + sum_cols(transposed(whole_grad_qkv, qkv_w))
    grad_qkv_w = outer_sum(whole_tokens, whole_grad_qkv)
    weight_parts = (
        grad_qkv_w[:, :width_col],
        grad_qkv_w[:, width_col : 2 * width_col],
        grad_qkv_w[:, 2 * width_col :],
        grad_w_attn_out,
        grad_w_inter,
        grad_w_ffout,
    )
    vector_parts = (
        placed(grad_b_query, col_start, D),
        placed(grad_b_value, col_start, D),
        placed(grad_b_attn_out, row_start, D),
        placed(grad_b_inter, ff_start, FF),
        placed(grad_b_ffout, row_start, D),
        placed(grad_gain_one, row_start, D),
        placed(grad_shift_one, row_start, D),
        placed(grad_gain_two, row_start, D),
        placed(grad_shift_two, row_start, D),
    )
    return (layer_out.astype(jnp.bfloat16), grad_tokens, weight_parts, vector_parts)


def per_device(
    tokens,
    w_query,
    w_key,
    w_value,
    w_attn_out,
    w_inter,
    w_ffout,
    b_query,
    b_value,
    b_attn_out,
    b_inter,
    b_ffout,
    gain_one,
    shift_one,
    gain_two,
    shift_two,
    lengths,
    block_order,
    cotangent,
):
    weights = (w_query, w_key, w_value, w_attn_out, w_inter, w_ffout)
    vectors = (
        b_query,
        b_value,
        b_attn_out,
        b_inter,
        b_ffout,
        gain_one,
        shift_one,
        gain_two,
        shift_two,
    )
    results = grid_plan(tokens, weights, vectors, lengths, block_order, cotangent)
    layer_out, grad_tokens, weight_parts, vector_parts = results
    grad_w_query, grad_w_key, grad_w_value, grad_w_attn_out, grad_w_inter, grad_w_ffout = (
        lax.psum(weight_parts[0].astype(jnp.bfloat16), "dp").astype(jnp.float32),
        lax.psum(weight_parts[1].astype(jnp.bfloat16), "dp").astype(jnp.float32),
        lax.psum(weight_parts[2].astype(jnp.bfloat16), "dp").astype(jnp.float32),
        lax.psum(weight_parts[3].astype(jnp.bfloat16), "dp").astype(jnp.float32),
        lax.psum(weight_parts[4].astype(jnp.bfloat16), "dp").astype(jnp.float32),
        lax.psum(weight_parts[5].astype(jnp.bfloat16), "dp").astype(jnp.float32),
    )
    (
        grad_b_query,
        grad_b_value,
        grad_b_attn_out,
        grad_b_inter,
        grad_b_ffout,
        grad_gain_one,
        grad_shift_one,
        grad_gain_two,
        grad_shift_two,
    ) = lax.psum(
        (
            vector_parts[0],
            vector_parts[1],
            vector_parts[2],
            vector_parts[3],
            vector_parts[4],
            vector_parts[5],
            vector_parts[6],
            vector_parts[7],
            vector_parts[8],
        ),
        ("dp", "row", "col"),
    )
    return (
        layer_out,
        grad_tokens,
        grad_w_query,
        grad_w_key,
        grad_w_value,
        grad_w_attn_out,
        grad_w_inter,
        grad_w_ffout,
        grad_b_query,
        grad_b_value,
        grad_b_attn_out,
        grad_b_inter,
        grad_b_ffout,
        grad_gain_one,
        grad_shift_one,
        grad_gain_two,
        grad_shift_two,
    )


def solution(mesh):
    return jax.shard_map(
        per_device,
        mesh=mesh,
        in_specs=(
            P(("dp", "col"), "row"),
            P("row", "col"),
            P("row", "col"),
            P("row", "col"),
            P("col", "row"),
            P("row", "col"),
            P("col", "row"),
            P(),
            P(),
            P(),
            P(),
            P(),
            P(),
            P(),
            P(),
            P(),
            P(),
            P(),
            P(("dp", "col"), "row"),
        ),
        out_specs=(
            P(("dp", "col"), "row"),
            P(("dp", "col"), "row"),
            P("row", "col"),
            P("row", "col"),
            P("row", "col"),
            P("col", "row"),
            P("row", "col"),
            P("col", "row"),
            P(),
            P(),
            P(),
            P(),
            P(),
            P(),
            P(),
            P(),
            P(),
        ),
        check_vma=False,
    )
```

profile of v0, /device:TPU:0, one launch (start us, length us, event | category | flops | bytes accessed | tf_op | source)
XLA Modules:
  0.0 1184.7 jit_solution(4707898755306142605)
XLA Ops:
  10.4 46.9 %all-gather.9.cloned.1.call-done = bf16[4096,384]{1,0:T(8,128)(2,1)} async-done(((bf16[2048,384]{1,0:T(8,128)(2,1)}), bf16[4096,384]{1,0:T(8,128)(2,1)}) %all-gather.9.cloned.1.call-update) | async-done | bytes 3145744 | tf_op jit(solution)/shard_map/all_gather | solution.py:39
  69.7 27.0 %reduce-scatter.9.cloned.1.call-done = f32[2048,1152]{0,1:T(8,128)} async-done(((f32[4096,1152]{0,1:T(8,128)}), f32[2048,1152]{0,1:T(8,128)}) %reduce-scatter.9.cloned.1.call-update) | async-done | bytes 9437200 | tf_op jit(solution)/shard_map/reduce_scatter | solution.py:47
  108.7 84.4 %while.38 = (s32[]{:T(128)}, bf16[2048,384]{0,1:T(8,128)(2,1)}, f32[2048,6]{0,1:T(8,128)S(1)}, s32[6,2]{0,1:T(2,128)S(1)}, s32[1]{0:T(128)}, /*index=5*/bf16[204...) while((s32[]{:T(128)}, bf16[2048,384]{0,1:T(8,128)(2,1)}, ...), condition=%wide.region_4.5_spmd, body=%wide.region_1.4_spmd.sunk | while | flops 281019456 | bytes 13681410 | solution.py:133
  193.2 13.5 %all-gather.11.cloned.1.call-done = bf16[4096,384]{0,1:T(8,128)(2,1)} async-done(((bf16[2048,384]{0,1:T(8,128)(2,1)}), bf16[4096,384]{0,1:T(8,128)(2,1)}) %all-gather.11.cloned.1.call-update) | async-done | bytes 3145744 | tf_op jit(solution)/shard_map/all_gather | solution.py:43
  213.5 43.8 %reduce-scatter.11.cloned.1.call-done = bf16[2048,384]{1,0:T(8,128)(2,1)} async-done(((bf16[4096,384]{1,0:T(8,128)(2,1)}), bf16[2048,384]{1,0:T(8,128)(2,1)}) %reduce-scatter.11.cloned.1.call-update) | async-done | bytes 1572880 | tf_op jit(solution)/shard_map/reduce_scatter | solution.py:51
  265.2 44.9 %all-gather.13.cloned.1.call-done = bf16[4096,384]{1,0:T(8,128)(2,1)} async-done(((bf16[2048,384]{1,0:T(8,128)(2,1)}), bf16[4096,384]{1,0:T(8,128)(2,1)}) %all-gather.13.cloned.1.call-update) | async-done | bytes 3145744 | tf_op jit(solution)/shard_map/all_gather | solution.py:39
  310.1 13.8 %fusion.62 = f32[4096,1536]{1,0:T(8,128)} fusion(bf16[4096,384]{1,0:T(8,128)(2,1)} %all-gather.13.cloned.1.call-done, f32[384,1536]{1,0:T(8,128)} %param.28), kind=kOutput, calls=%fused_computation.116 | convolution fusion | flops 4832428032 | bytes 30670848 | tf_op jit(solution)/shard_map/dot_general | solution.py:15
  324.7 34.9 %reduce-scatter.13.cloned.1.call-done = f32[2048,1536]{1,0:T(8,128)} async-done(((f32[4096,1536]{1,0:T(8,128)}), f32[2048,1536]{1,0:T(8,128)}) %reduce-scatter.13.cloned.1.call-update) | async-done | bytes 12582928 | tf_op jit(solution)/shard_map/reduce_scatter | solution.py:47
  359.6 30.2 %multiply_convert_fusion.1 = (bf16[2048,1536]{1,0:T(8,128)(2,1)}, f32[2048,1536]{1,0:T(8,128)}) fusion(f32[2048,1536]{1,0:T(8,128)} %reduce-scatter.13.cloned.1.call-done, f32[1536]{0:T(1024)S(1)} %dynamic_slice.159), kind=kLoop, calls=%fused_computation.53 | loop fusion | flops 207618048 | bytes 31463424 | tf_op jit(solution)/shard_map/convert_element_type | solution.py:244
  389.8 26.2 %all-gather.15.cloned.1.call-done = bf16[4096,1536]{1,0:T(8,128)(2,1)} async-done(((bf16[2048,1536]{1,0:T(8,128)(2,1)}), bf16[4096,1536]{1,0:T(8,128)(2,1)}) %all-gather.15.cloned.1.call-update) | async-done | bytes 12582928 | tf_op jit(solution)/shard_map/all_gather | solution.py:43
  429.0 43.2 %reduce-scatter.15.cloned.1.call-done = bf16[2048,384]{1,0:T(8,128)(2,1)} async-done(((bf16[4096,384]{1,0:T(8,128)(2,1)}), bf16[2048,384]{1,0:T(8,128)(2,1)}) %reduce-scatter.15.cloned.1.call-update) | async-done | bytes 1572880 | tf_op jit(solution)/shard_map/reduce_scatter | solution.py:51
  493.6 44.8 %all-gather.17.cloned.1.call-done = bf16[4096,384]{1,0:T(8,128)(2,1)} async-done(((bf16[2048,384]{1,0:T(8,128)(2,1)}), bf16[4096,384]{1,0:T(8,128)(2,1)}) %all-gather.17.cloned.1.call-update) | async-done | bytes 3145744 | tf_op jit(solution)/shard_map/all_gather | solution.py:39
  538.5 13.8 %fusion.58 = f32[4096,1536]{1,0:T(8,128)} fusion(bf16[4096,384]{1,0:T(8,128)(2,1)} %all-gather.17.cloned.1.call-done, f32[1536,384]{1,0:T(8,128)} %param.29), kind=kOutput, calls=%fused_computation.112 | convolution fusion | flops 4832428032 | bytes 30670848 | tf_op jit(solution)/shard_map/dot_general | solution.py:19
  552.4 35.5 %reduce-scatter.17.cloned.1.call-done = f32[2048,1536]{1,0:T(8,128)} async-done(((f32[4096,1536]{1,0:T(8,128)}), f32[2048,1536]{1,0:T(8,128)}) %reduce-scatter.17.cloned.1.call-update) | async-done | bytes 12582928 | tf_op jit(solution)/shard_map/reduce_scatter | solution.py:47
  587.9 17.0 %convert_reduce_fusion = (f32[1536]{0:T(1024)S(1)}, bf16[2048,1536]{1,0:T(8,128)(2,1)}) fusion(f32[2048,1536]{1,0:T(8,128)} %reduce-scatter.17.cloned.1.call-done, f32[2048,1536]{1,0:T(8,128)} %get-tuple-element.691, f32[2048,1536]{1,0:T(8,128)} %reduce-scatter.13.cloned.1.call-done, f32[1536]{0:T(1024)S(1)} %dynamic_slice.159), kind=kLoop, calls=%fused_computation.51 | loop fusion | flops 53475840 | bytes 44052480 | tf_op jit(solution)/shard_map/reduce_sum | solution.py:259
  605.0 26.2 %all-gather.19.cloned.1.call-done = bf16[4096,1536]{1,0:T(8,128)(2,1)} async-done(((bf16[2048,1536]{1,0:T(8,128)(2,1)}), bf16[4096,1536]{1,0:T(8,128)(2,1)}) %all-gather.19.cloned.1.call-update) | async-done | bytes 12582928 | tf_op jit(solution)/shard_map/all_gather | solution.py:43
  631.2 11.6 convolution_convert_fusion.2
  642.8 44.6 %reduce-scatter.19.cloned.1.call-done = bf16[2048,384]{1,0:T(8,128)(2,1)} async-done(((bf16[4096,384]{1,0:T(8,128)(2,1)}), bf16[2048,384]{1,0:T(8,128)(2,1)}) %reduce-scatter.19.cloned.1.call-update) | async-done | bytes 1572880 | tf_op jit(solution)/shard_map/reduce_scatter | solution.py:51
  701.8 44.8 %all-gather.21.cloned.1.call-done = bf16[4096,384]{1,0:T(8,128)(2,1)} async-done(((bf16[2048,384]{1,0:T(8,128)(2,1)}), bf16[4096,384]{1,0:T(8,128)(2,1)}) %all-gather.21.cloned.1.call-update) | async-done | bytes 3145744 | tf_op jit(solution)/shard_map/all_gather | solution.py:39
  753.3 14.6 %reduce-scatter.21.cloned.1.call-done = f32[2048,384]{1,0:T(8,128)} async-done(((f32[4096,384]{1,0:T(8,128)}), f32[2048,384]{1,0:T(8,128)}) %reduce-scatter.21.cloned.1.call-update) | async-done | bytes 3145744 | tf_op jit(solution)/shard_map/reduce_scatter | solution.py:47
  772.8 175.0 %while.39 = (s32[]{:T(128)}, bf16[2048,384]{0,1:T(8,128)(2,1)S(1)}, bf16[1,2048,384]{1,2,0:T(8,128)(2,1)}, bf16[1,2048,384]{1,2,0:T(8,128)(2,1)S(1)}, s32[6,2]{0...) while((s32[]{:T(128)}, bf16[2048,384]{0,1:T(8,128)(2,1)S(1)}, ...), condition=%wide.region_29.30_spmd, body=%wide.region_27.29_spmd.sunk | while | flops 687866944 | bytes 34122520 | solution.py:183
  999.2 45.3 %all-reduce = (f32[768]{0:T(1024)}, f32[768]{0:T(1024)}, f32[768]{0:T(1024)}, f32[3072]{0:T(1024)}, f32[768]{0:T(1024)}, /*index=5*/f32[768]{0:T(1024)}, f32[768]{0:T(1024)}, f32[768]{0:T(1024)}, f32[768]{0:T(1024)}) all-reduce(f32[768]{0:T(1024)S(1)} %dynamic_update_slice.82, ...), channel_id=1, replica_groups=mesh['dp'=8,'row'=2,'col'=2] {'dp','row','col'}, use_global_device_ids=true, to_apply=%region_38.39 | all-reduce | flops 9216 | bytes 73728 | tf_op jit(solution)/shard_map/psum | solution.py:370
  1044.5 85.6 %all-reduce.8.cloned.1.call-done = (bf16[384,384]{0,1:T(8,128)(2,1)}, bf16[384,384]{0,1:T(8,128)(2,1)}, bf16[384,384]{0,1:T(8,128)(2,1)}, bf16[384,384]{1,0:T(8,...) async-done(((bf16[384,384]{0,1:T(8,128)(2,1)}, bf16[384,384]{0,1:T(8,128)(2,1)}, bf16[384,384]{0,1:T(8,128)(2,1)}, bf16[384,384]{1,0:T(8,128)(2,1)}, ...) | async-done | bytes 3538960 | tf_op jit(solution)/shard_map/psum | solution.py:353
  1143.9 30.6 %reduce-scatter.23.cloned.1.call-done = bf16[2048,384]{1,0:T(8,128)(2,1)} async-done(((bf16[4096,384]{1,0:T(8,128)(2,1)}), bf16[2048,384]{1,0:T(8,128)(2,1)}) %reduce-scatter.23.cloned.1.call-update) | async-done | bytes 1572880 | tf_op jit(solution)/shard_map/reduce_scatter | solution.py:51
  (366 shorter events, 412.8 us)
Async XLA Ops:
  7.2 62.4 %copy-start = (s32[12,2]{0,1:T(2,128)S(1)}, s32[12,2]{0,1:T(2,128)}, u32[]{:S(2)}) copy-start(s32[12,2]{0,1:T(2,128)} %param.40) | copy-start | bytes 292
  7.2 50.0 %all-gather.9.cloned.1.call-start = ((), (), s32[]{:S(2)}) async-start(), calls=%async_computation.8 | async-start | bytes 4718592 | tf_op jit(solution)/shard_map/all_gather | solution.py:39
  8.0 88.7 %reduce-scatter.9.cloned.1.call-start = ((), (), s32[]{:S(2)}) async-start(), calls=%async_computation.9 | async-start | bytes 28311552 | tf_op jit(solution)/shard_map/reduce_scatter | solution.py:47
  9.1 59.0 %copy-start.10 = (bf16[384,384]{1,0:T(8,128)(2,1)}, bf16[384,384]{1,0:T(8,128)(2,1)S(1)}, u32[]{:S(2)}) copy-start(bf16[384,384]{1,0:T(8,128)(2,1)S(1)} %convert_element_type.176) | copy-start | bytes 884740
  10.3 57.8 %copy-start.12 = (bf16[384,384]{1,0:T(8,128)(2,1)}, bf16[384,384]{1,0:T(8,128)(2,1)S(1)}, u32[]{:S(2)}) copy-start(bf16[384,384]{1,0:T(8,128)(2,1)S(1)} %convert_element_type.177) | copy-start | bytes 884740
  10.4 57.8 %copy-start.13 = (bf16[384,384]{1,0:T(8,128)(2,1)}, bf16[384,384]{1,0:T(8,128)(2,1)S(1)}, u32[]{:S(2)}) copy-start(bf16[384,384]{1,0:T(8,128)(2,1)S(1)} %convert_element_type.178) | copy-start | bytes 884740
  68.2 138.6 %all-gather.11.cloned.1.call-start = ((), (), s32[]{:S(2)}) async-start(), calls=%async_computation.10 | async-start | bytes 4718592 | tf_op jit(solution)/shard_map/all_gather | solution.py:43
  193.2 64.2 %reduce-scatter.11.cloned.1.call-start = ((), (), s32[]{:S(2)}) async-start(), calls=%async_computation.11 | async-start | bytes 4718592 | tf_op jit(solution)/shard_map/reduce_scatter | solution.py:51
  212.6 44.7 %copy-start.2 = (bf16[2048,384]{1,0:T(8,128)(2,1)S(1)}, bf16[2048,384]{1,0:T(8,128)(2,1)}, u32[]{:S(2)}) copy-start(bf16[2048,384]{1,0:T(8,128)(2,1)} %param.23) | copy-start | bytes 4718596
  212.7 97.5 %all-gather.13.cloned.1.call-start = ((), (), s32[]{:S(2)}) async-start(), calls=%async_computation.12 | async-start | bytes 4718592 | tf_op jit(solution)/shard_map/all_gather | solution.py:39
  265.0 94.6 %reduce-scatter.13.cloned.1.call-start = ((), (), s32[]{:S(2)}) async-start(), calls=%async_computation.13 | async-start | bytes 37748736 | tf_op jit(solution)/shard_map/reduce_scatter | solution.py:47
  323.9 92.0 %all-gather.15.cloned.1.call-start = ((), (), s32[]{:S(2)}) async-start(), calls=%async_computation.14 | async-start | bytes 18874368 | tf_op jit(solution)/shard_map/all_gather | solution.py:43
  389.8 82.4 %reduce-scatter.15.cloned.1.call-start = ((), (), s32[]{:S(2)}) async-start(), calls=%async_computation.15 | async-start | bytes 4718592 | tf_op jit(solution)/shard_map/reduce_scatter | solution.py:51
  427.5 111.0 %all-gather.17.cloned.1.call-start = ((), (), s32[]{:S(2)}) async-start(), calls=%async_computation.16 | async-start | bytes 4718592 | tf_op jit(solution)/shard_map/all_gather | solution.py:39
  493.4 94.6 %reduce-scatter.17.cloned.1.call-start = ((), (), s32[]{:S(2)}) async-start(), calls=%async_computation.17 | async-start | bytes 37748736 | tf_op jit(solution)/shard_map/reduce_scatter | solution.py:47
  552.3 78.8 %all-gather.19.cloned.1.call-start = ((), (), s32[]{:S(2)}) async-start(), calls=%async_computation.18 | async-start | bytes 18874368 | tf_op jit(solution)/shard_map/all_gather | solution.py:43
  604.9 82.5 %reduce-scatter.19.cloned.1.call-start = ((), (), s32[]{:S(2)}) async-start(), calls=%async_computation.19 | async-start | bytes 4718592 | tf_op jit(solution)/shard_map/reduce_scatter | solution.py:51
  642.8 103.9 %all-gather.21.cloned.1.call-start = ((), (), s32[]{:S(2)}) async-start(), calls=%async_computation.20 | async-start | bytes 4718592 | tf_op jit(solution)/shard_map/all_gather | solution.py:39
  700.2 46.4 %copy-start.14 = (f32[384,384]{1,0:T(8,128)S(1)}, f32[384,384]{1,0:T(8,128)}, u32[]{:S(2)}) copy-start(f32[384,384]{1,0:T(8,128)} %param.27) | copy-start | bytes 1769476
  701.5 66.3 %reduce-scatter.21.cloned.1.call-start = ((), (), s32[]{:S(2)}) async-start(), calls=%async_computation.21 | async-start | bytes 9437184 | tf_op jit(solution)/shard_map/reduce_scatter | solution.py:47
  753.2 223.6 %all-gather.23.cloned.1.call-start = ((), (), s32[]{:S(2)}) async-start(), calls=%async_computation.22 | async-start | bytes 14155776 | tf_op jit(solution)/shard_map/all_gather | solution.py:43
  951.6 178.6 %all-reduce.8.cloned.1.call-start = ((), (), s32[]{:S(2)}) async-start(), calls=%async_computation.24 | async-start | bytes 7077888 | tf_op jit(solution)/shard_map/psum | solution.py:353
  986.4 188.2 %reduce-scatter.23.cloned.1.call-start = ((), (), s32[]{:S(2)}) async-start(), calls=%async_computation.23 | async-start | bytes 4718592 | tf_op jit(solution)/shard_map/reduce_scatter | solution.py:51
  1141.1 36.9 %copy-start.1 = (s32[12,2]{0,1:T(2,128)S(1)}, s32[12,2]{0,1:T(2,128)}, u32[]{:S(2)}) copy-start(s32[12,2]{0,1:T(2,128)} %param.40) | copy-start | bytes 292
  (22 other events, 123.4 us)
Sparse Core Ops, SparseCore 0:
  9.6 47.6 all-gather.8
  68.3 28.2 reduce-scatter.8
  193.3 13.4 all-gather.10
  212.8 44.5 reduce-scatter.10
  265.1 44.9 all-gather.12
  324.1 35.4 reduce-scatter.12
  389.9 26.0 all-gather.14
  427.6 44.5 reduce-scatter.14
  493.5 44.9 all-gather.16
  552.5 35.4 reduce-scatter.16
  605.1 26.0 all-gather.18
  642.9 44.5 reduce-scatter.18
  701.7 44.9 all-gather.20
  753.3 14.4 reduce-scatter.20
  951.7 23.0 all-gather.22
  986.5 143.6 all-reduce.7
  1132.3 42.1 reduce-scatter.22
where the time goes:
time: 1200 us; the launch traced here: 1180 us
  waiting for transfers between devices  608 us (51%)
  matrix products  291 us (24%)
  other arithmetic  148 us (12%)
  blocking collectives  58.6 us (5%)
  local copies, waits for them, and re-layouts  43.4 us (4%)
  loops' own time  18.5 us (2%)
  between operations  14.5 us (1%)
    all_gather x4, waiting for transfers between devices, gather_cols(): return lax.all_gather(values, 'col', axis=0, tiled=True)  181 us
    reduce_scatter x4, waiting for transfers between devices, sum_cols(): lax.psum_scatter(values.astype(jnp.bfloat16), 'col', scatter_dimension=0,...  162 us
    reduce_scatter x4, waiting for transfers between devices, sum_rows(): return lax.psum_scatter(values, 'row', scatter_dimension=0, tiled=True)  112 us
    dot_general x40, matrix products, transposed(): lax.dot_general(left, right, (((1,), (1,)), ((), ())), preferred_element_...  106 us
    dot_general x28, matrix products, product(): return jnp.dot(left, right, preferred_element_type=jnp.float32)  96.1 us
    dot_general x28, matrix products, outer_sum(): lax.dot_general(left, right, (((0,), (0,)), ((), ())), preferred_element_...  88.9 us
    psum x1, waiting for transfers between devices, per_device(): lax.psum(weight_parts[0].astype(jnp.bfloat16), 'dp').astype(jnp.float32)  85.6 us
    all_gather x4, waiting for transfers between devices, gather_rows(): return lax.all_gather(values, 'row', axis=0, tiled=True)  65.9 us
  transfers between devices with their start and end apart: 17, of which 16 were waited for; matrix products, arithmetic and copies ran while one was open for 5% of the time, Pallas kernels for 0%

commit v1 on v0

--- a/solution.py
+++ b/solution.py
@@ -1,3 +1,4 @@
+import functools
 import jax
 import jax.numpy as jnp
 from jax import lax
@@ -9,6 +10,13 @@
 SEQ = 2048
 eps_norm = 1e-05
 masked_score = -1e30
+
+
+def post_run(field, net_axis):
+    return jnp.sum(lax.all_gather(field, net_axis), axis=0)
+
+
+fill_the_pipes = functools.partial(post_run, net_axis="dp")
 
 
 def product(left, right):
@@ -350,7 +358,7 @@
     results = grid_plan(tokens, weights, vectors, lengths, block_order, cotangent)
     layer_out, grad_tokens, weight_parts, vector_parts = results
     grad_w_query, grad_w_key, grad_w_value, grad_w_attn_out, grad_w_inter, grad_w_ffout = (
-        lax.psum(weight_parts[0].astype(jnp.bfloat16), "dp").astype(jnp.float32),
+        fill_the_pipes(weight_parts[0].astype(jnp.bfloat16)).astype(jnp.float32),
         lax.psum(weight_parts[1].astype(jnp.bfloat16), "dp").astype(jnp.float32),
         lax.psum(weight_parts[2].astype(jnp.bfloat16), "dp").astype(jnp.float32),
         lax.psum(weight_parts[3].astype(jnp.bfloat16), "dp").astype(jnp.float32),

time: 1200 us -> 1240 us (1.033)
  waiting for transfers between devices: 608 us -> 654 us
    all_gather x0 -> x1, waiting for transfers between devices: none -> 45.4 us  [post_run(): return jnp.sum(lax.all_gather(field, net_axis), axis=0)]
  transfers between devices with their start and end apart: 17 -> 18, of which waited for: 16 -> 17; matrix products, arithmetic and copies ran while one was open for 5% -> 4% of each run, Pallas kernels for 0% -> 0%
where the time goes in v1:
time: 1240 us; the launch traced here: 1230 us
  waiting for transfers between devices  654 us (53%)
  matrix products  291 us (23%)
  other arithmetic  147 us (12%)
  blocking collectives  57.8 us (5%)
  local copies, waits for them, and re-layouts  44.9 us (4%)
  loops' own time  18.5 us (1%)
  between operations  15.1 us (1%)
    all_gather x4, waiting for transfers between devices, gather_cols(): return lax.all_gather(values, 'col', axis=0, tiled=True)  181 us
    reduce_scatter x4, waiting for transfers between devices, sum_cols(): lax.psum_scatter(values.astype(jnp.bfloat16), 'col', scatter_dimension=0,...  170 us
    reduce_scatter x4, waiting for transfers between devices, sum_rows(): return lax.psum_scatter(values, 'row', scatter_dimension=0, tiled=True)  112 us
    dot_general x40, matrix products, transposed(): lax.dot_general(left, right, (((1,), (1,)), ((), ())), preferred_element_...  106 us
    dot_general x28, matrix products, product(): return jnp.dot(left, right, preferred_element_type=jnp.float32)  96.1 us
    dot_general x28, matrix products, outer_sum(): lax.dot_general(left, right, (((0,), (0,)), ((), ())), preferred_element_...  88.8 us
    psum x1, waiting for transfers between devices, per_device(): lax.psum(weight_parts[1].astype(jnp.bfloat16), 'dp').astype(jnp.float32)  78.1 us
    all_gather x4, waiting for transfers between devices, gather_rows(): return lax.all_gather(values, 'row', axis=0, tiled=True)  65.8 us
  transfers between devices with their start and end apart: 18, of which 17 were waited for; matrix products, arithmetic and copies ran while one was open for 4% of the time, Pallas kernels for 0%

profile of v1, /device:TPU:0, one launch (start us, length us, event | category | flops | bytes accessed | tf_op | source)
XLA Modules:
  0.0 1231.1 jit_solution(8092135030662211717)
XLA Ops:
  10.4 46.9 %all-gather.11.cloned.1.call-done = bf16[4096,384]{1,0:T(8,128)(2,1)} async-done(((bf16[2048,384]{1,0:T(8,128)(2,1)}), bf16[4096,384]{1,0:T(8,128)(2,1)}) %all-gather.11.cloned.1.call-update) | async-done | bytes 3145744 | tf_op jit(solution)/shard_map/all_gather | solution.py:47
  69.7 27.0 %reduce-scatter.9.cloned.1.call-done = f32[2048,1152]{0,1:T(8,128)} async-done(((f32[4096,1152]{0,1:T(8,128)}), f32[2048,1152]{0,1:T(8,128)}) %reduce-scatter.9.cloned.1.call-update) | async-done | bytes 9437200 | tf_op jit(solution)/shard_map/reduce_scatter | solution.py:55
  108.8 84.4 %while.38 = (s32[]{:T(128)}, bf16[2048,384]{0,1:T(8,128)(2,1)}, f32[2048,6]{0,1:T(8,128)S(1)}, s32[6,2]{0,1:T(2,128)S(1)}, s32[1]{0:T(128)}, /*index=5*/bf16[204...) while((s32[]{:T(128)}, bf16[2048,384]{0,1:T(8,128)(2,1)}, ...), condition=%wide.region_4.5_spmd, body=%wide.region_1.4_spmd.sunk | while | flops 281019456 | bytes 13681410 | solution.py:141
  193.3 13.5 %all-gather.13.cloned.1.call-done = bf16[4096,384]{0,1:T(8,128)(2,1)} async-done(((bf16[2048,384]{0,1:T(8,128)(2,1)}), bf16[4096,384]{0,1:T(8,128)(2,1)}) %all-gather.13.cloned.1.call-update) | async-done | bytes 3145744 | tf_op jit(solution)/shard_map/all_gather | solution.py:51
  213.5 43.8 %reduce-scatter.11.cloned.1.call-done = bf16[2048,384]{1,0:T(8,128)(2,1)} async-done(((bf16[4096,384]{1,0:T(8,128)(2,1)}), bf16[2048,384]{1,0:T(8,128)(2,1)}) %reduce-scatter.11.cloned.1.call-update) | async-done | bytes 1572880 | tf_op jit(solution)/shard_map/reduce_scatter | solution.py:59
  265.3 44.8 %all-gather.15.cloned.1.call-done = bf16[4096,384]{1,0:T(8,128)(2,1)} async-done(((bf16[2048,384]{1,0:T(8,128)(2,1)}), bf16[4096,384]{1,0:T(8,128)(2,1)}) %all-gather.15.cloned.1.call-update) | async-done | bytes 3145744 | tf_op jit(solution)/shard_map/all_gather | solution.py:47
  310.1 13.8 %fusion.62 = f32[4096,1536]{1,0:T(8,128)} fusion(bf16[4096,384]{1,0:T(8,128)(2,1)} %all-gather.15.cloned.1.call-done, f32[384,1536]{1,0:T(8,128)} %param.28), kind=kOutput, calls=%fused_computation.117 | convolution fusion | flops 4832428032 | bytes 30670848 | tf_op jit(solution)/shard_map/dot_general | solution.py:23
  324.7 34.9 %reduce-scatter.13.cloned.1.call-done = f32[2048,1536]{1,0:T(8,128)} async-done(((f32[4096,1536]{1,0:T(8,128)}), f32[2048,1536]{1,0:T(8,128)}) %reduce-scatter.13.cloned.1.call-update) | async-done | bytes 12582928 | tf_op jit(solution)/shard_map/reduce_scatter | solution.py:55
  359.6 30.2 %multiply_convert_fusion.1 = (bf16[2048,1536]{1,0:T(8,128)(2,1)}, f32[2048,1536]{1,0:T(8,128)}) fusion(f32[2048,1536]{1,0:T(8,128)} %reduce-scatter.13.cloned.1.call-done, f32[1536]{0:T(1024)S(1)} %dynamic_slice.159), kind=kLoop, calls=%fused_computation.53 | loop fusion | flops 207618048 | bytes 31463424 | tf_op jit(solution)/shard_map/convert_element_type | solution.py:252
  389.8 26.2 %all-gather.17.cloned.1.call-done = bf16[4096,1536]{1,0:T(8,128)(2,1)} async-done(((bf16[2048,1536]{1,0:T(8,128)(2,1)}), bf16[4096,1536]{1,0:T(8,128)(2,1)}) %all-gather.17.cloned.1.call-update) | async-done | bytes 12582928 | tf_op jit(solution)/shard_map/all_gather | solution.py:51
  429.1 43.2 %reduce-scatter.15.cloned.1.call-done = bf16[2048,384]{1,0:T(8,128)(2,1)} async-done(((bf16[4096,384]{1,0:T(8,128)(2,1)}), bf16[2048,384]{1,0:T(8,128)(2,1)}) %reduce-scatter.15.cloned.1.call-update) | async-done | bytes 1572880 | tf_op jit(solution)/shard_map/reduce_scatter | solution.py:59
  493.9 44.6 %all-gather.19.cloned.1.call-done = bf16[4096,384]{1,0:T(8,128)(2,1)} async-done(((bf16[2048,384]{1,0:T(8,128)(2,1)}), bf16[4096,384]{1,0:T(8,128)(2,1)}) %all-gather.19.cloned.1.call-update) | async-done | bytes 3145744 | tf_op jit(solution)/shard_map/all_gather | solution.py:47
  538.5 13.8 %fusion.58 = f32[4096,1536]{1,0:T(8,128)} fusion(bf16[4096,384]{1,0:T(8,128)(2,1)} %all-gather.19.cloned.1.call-done, f32[1536,384]{1,0:T(8,128)} %param.29), kind=kOutput, calls=%fused_computation.113 | convolution fusion | flops 4832428032 | bytes 30670848 | tf_op jit(solution)/shard_map/dot_general | solution.py:27
  552.4 35.5 %reduce-scatter.17.cloned.1.call-done = f32[2048,1536]{1,0:T(8,128)} async-done(((f32[4096,1536]{1,0:T(8,128)}), f32[2048,1536]{1,0:T(8,128)}) %reduce-scatter.17.cloned.1.call-update) | async-done | bytes 12582928 | tf_op jit(solution)/shard_map/reduce_scatter | solution.py:55
  588.0 17.0 %convert_reduce_fusion = (f32[1536]{0:T(1024)S(1)}, bf16[2048,1536]{1,0:T(8,128)(2,1)}) fusion(f32[2048,1536]{1,0:T(8,128)} %reduce-scatter.17.cloned.1.call-done, f32[2048,1536]{1,0:T(8,128)} %get-tuple-element.726, f32[2048,1536]{1,0:T(8,128)} %reduce-scatter.13.cloned.1.call-done, f32[1536]{0:T(1024)S(1)} %dynamic_slice.159), kind=kLoop, calls=%fused_computation.51 | loop fusion | flops 53475840 | bytes 44052480 | tf_op jit(solution)/shard_map/reduce_sum | solution.py:267
  605.0 26.2 %all-gather.21.cloned.1.call-done = bf16[4096,1536]{1,0:T(8,128)(2,1)} async-done(((bf16[2048,1536]{1,0:T(8,128)(2,1)}), bf16[4096,1536]{1,0:T(8,128)(2,1)}) %all-gather.21.cloned.1.call-update) | async-done | bytes 12582928 | tf_op jit(solution)/shard_map/all_gather | solution.py:51
  642.9 44.6 %reduce-scatter.19.cloned.1.call-done = bf16[2048,384]{1,0:T(8,128)(2,1)} async-done(((bf16[4096,384]{1,0:T(8,128)(2,1)}), bf16[2048,384]{1,0:T(8,128)(2,1)}) %reduce-scatter.19.cloned.1.call-update) | async-done | bytes 1572880 | tf_op jit(solution)/shard_map/reduce_scatter | solution.py:59
  701.8 44.9 %all-gather.23.cloned.1.call-done = bf16[4096,384]{1,0:T(8,128)(2,1)} async-done(((bf16[2048,384]{1,0:T(8,128)(2,1)}), bf16[4096,384]{1,0:T(8,128)(2,1)}) %all-gather.23.cloned.1.call-update) | async-done | bytes 3145744 | tf_op jit(solution)/shard_map/all_gather | solution.py:47
  753.4 14.6 %reduce-scatter.21.cloned.1.call-done = f32[2048,384]{1,0:T(8,128)} async-done(((f32[4096,384]{1,0:T(8,128)}), f32[2048,384]{1,0:T(8,128)}) %reduce-scatter.21.cloned.1.call-update) | async-done | bytes 3145744 | tf_op jit(solution)/shard_map/reduce_scatter | solution.py:55
  772.9 175.0 %while.39 = (s32[]{:T(128)}, bf16[2048,384]{0,1:T(8,128)(2,1)S(1)}, bf16[1,2048,384]{1,2,0:T(8,128)(2,1)}, bf16[1,2048,384]{1,2,0:T(8,128)(2,1)S(1)}, s32[6,2]{0...) while((s32[]{:T(128)}, bf16[2048,384]{0,1:T(8,128)(2,1)S(1)}, ...), condition=%wide.region_29.30_spmd, body=%wide.region_27.29_spmd.sunk | while | flops 687866944 | bytes 34122520 | solution.py:191
  999.6 44.5 %all-reduce = (f32[768]{0:T(1024)}, f32[768]{0:T(1024)}, f32[768]{0:T(1024)}, f32[3072]{0:T(1024)}, f32[768]{0:T(1024)}, /*index=5*/f32[768]{0:T(1024)}, f32[768]{0:T(1024)}, f32[768]{0:T(1024)}, f32[768]{0:T(1024)}) all-reduce(f32[768]{0:T(1024)S(1)} %dynamic_update_slice.82, ...), channel_id=1, replica_groups=mesh['dp'=8,'row'=2,'col'=2] {'dp','row','col'}, use_global_device_ids=true, to_apply=%region_38.39 | all-reduce | flops 9216 | bytes 73728 | tf_op jit(solution)/shard_map/psum | solution.py:378
  1044.1 78.1 %all-reduce.8.cloned.1.call-done = (bf16[384,384]{0,1:T(8,128)(2,1)}, bf16[384,384]{0,1:T(8,128)(2,1)}, bf16[384,384]{1,0:T(8,128)(2,1)}, bf16[384,1536]{1,0:T(8,128)(2,1)}, bf16[1536,384]{1,0:T(8,128)(2,1)}) async-done(((bf16[384,384]{0,1:T(8,128)(2,1)}, bf16[384,384]{0,1:T(8,128)(2,1)}, bf16[384,384]{1,0:T(8,128)(2,1)}, bf16[384,1536]{1,0:T(8,128)(2,1)}, bf16[1536,384]{1,0:T(8,128)(2,1)}), ...) | async-done | bytes 3244048 | tf_op jit(solution)/shard_map/psum | solution.py:362
  1131.3 45.4 %all-gather.27.cloned.1.call-done = bf16[3072,384]{0,1:T(8,128)(2,1)} async-done(((bf16[384,384]{0,1:T(8,128)(2,1)}), bf16[3072,384]{0,1:T(8,128)(2,1)}) %all-gather.27.cloned.1.call-update) | async-done | bytes 2359312 | tf_op jit(solution)/shard_map/all_gather | solution.py:16
  1181.9 38.5 %reduce-scatter.23.cloned.1.call-done = bf16[2048,384]{1,0:T(8,128)(2,1)} async-done(((bf16[4096,384]{1,0:T(8,128)(2,1)}), bf16[2048,384]{1,0:T(8,128)(2,1)}) %reduce-scatter.23.cloned.1.call-update) | async-done | bytes 1572880 | tf_op jit(solution)/shard_map/reduce_scatter | solution.py:59
  (375 shorter events, 425.3 us)
Async XLA Ops:
  7.2 62.4 %copy-start = (s32[12,2]{0,1:T(2,128)S(1)}, s32[12,2]{0,1:T(2,128)}, u32[]{:S(2)}) copy-start(s32[12,2]{0,1:T(2,128)} %param.40) | copy-start | bytes 292
  7.2 50.0 %all-gather.11.cloned.1.call-start = ((), (), s32[]{:S(2)}) async-start(), calls=%async_computation.8 | async-start | bytes 4718592 | tf_op jit(solution)/shard_map/all_gather | solution.py:47
  8.0 88.8 %reduce-scatter.9.cloned.1.call-start = ((), (), s32[]{:S(2)}) async-start(), calls=%async_computation.9 | async-start | bytes 28311552 | tf_op jit(solution)/shard_map/reduce_scatter | solution.py:55
  9.1 59.1 %copy-start.12 = (bf16[384,384]{1,0:T(8,128)(2,1)}, bf16[384,384]{1,0:T(8,128)(2,1)S(1)}, u32[]{:S(2)}) copy-start(bf16[384,384]{1,0:T(8,128)(2,1)S(1)} %convert_element_type.178) | copy-start | bytes 884740
  10.3 57.8 %copy-start.14 = (bf16[384,384]{1,0:T(8,128)(2,1)}, bf16[384,384]{1,0:T(8,128)(2,1)S(1)}, u32[]{:S(2)}) copy-start(bf16[384,384]{1,0:T(8,128)(2,1)S(1)} %convert_element_type.179) | copy-start | bytes 884740
  10.4 57.8 %copy-start.15 = (bf16[384,384]{1,0:T(8,128)(2,1)}, bf16[384,384]{1,0:T(8,128)(2,1)S(1)}, u32[]{:S(2)}) copy-start(bf16[384,384]{1,0:T(8,128)(2,1)S(1)} %convert_element_type.180) | copy-start | bytes 884740
  68.2 138.6 %all-gather.13.cloned.1.call-start = ((), (), s32[]{:S(2)}) async-start(), calls=%async_computation.10 | async-start | bytes 4718592 | tf_op jit(solution)/shard_map/all_gather | solution.py:51
  193.3 64.1 %reduce-scatter.11.cloned.1.call-start = ((), (), s32[]{:S(2)}) async-start(), calls=%async_computation.11 | async-start | bytes 4718592 | tf_op jit(solution)/shard_map/reduce_scatter | solution.py:59
  212.6 44.7 %copy-start.2 = (bf16[2048,384]{1,0:T(8,128)(2,1)S(1)}, bf16[2048,384]{1,0:T(8,128)(2,1)}, u32[]{:S(2)}) copy-start(bf16[2048,384]{1,0:T(8,128)(2,1)} %param.23) | copy-start | bytes 4718596
  212.7 97.5 %all-gather.15.cloned.1.call-start = ((), (), s32[]{:S(2)}) async-start(), calls=%async_computation.12 | async-start | bytes 4718592 | tf_op jit(solution)/shard_map/all_gather | solution.py:47
  265.0 94.6 %reduce-scatter.13.cloned.1.call-start = ((), (), s32[]{:S(2)}) async-start(), calls=%async_computation.13 | async-start | bytes 37748736 | tf_op jit(solution)/shard_map/reduce_scatter | solution.py:55
  324.0 92.0 %all-gather.17.cloned.1.call-start = ((), (), s32[]{:S(2)}) async-start(), calls=%async_computation.14 | async-start | bytes 18874368 | tf_op jit(solution)/shard_map/all_gather | solution.py:51
  389.8 82.4 %reduce-scatter.15.cloned.1.call-start = ((), (), s32[]{:S(2)}) async-start(), calls=%async_computation.15 | async-start | bytes 4718592 | tf_op jit(solution)/shard_map/reduce_scatter | solution.py:59
  427.5 111.0 %all-gather.19.cloned.1.call-start = ((), (), s32[]{:S(2)}) async-start(), calls=%async_computation.16 | async-start | bytes 4718592 | tf_op jit(solution)/shard_map/all_gather | solution.py:47
  493.4 94.6 %reduce-scatter.17.cloned.1.call-start = ((), (), s32[]{:S(2)}) async-start(), calls=%async_computation.17 | async-start | bytes 37748736 | tf_op jit(solution)/shard_map/reduce_scatter | solution.py:55
  552.4 78.8 %all-gather.21.cloned.1.call-start = ((), (), s32[]{:S(2)}) async-start(), calls=%async_computation.18 | async-start | bytes 18874368 | tf_op jit(solution)/shard_map/all_gather | solution.py:51
  605.0 82.5 %reduce-scatter.19.cloned.1.call-start = ((), (), s32[]{:S(2)}) async-start(), calls=%async_computation.19 | async-start | bytes 4718592 | tf_op jit(solution)/shard_map/reduce_scatter | solution.py:59
  642.8 103.9 %all-gather.23.cloned.1.call-start = ((), (), s32[]{:S(2)}) async-start(), calls=%async_computation.20 | async-start | bytes 4718592 | tf_op jit(solution)/shard_map/all_gather | solution.py:47
  700.3 46.4 %copy-start.16 = (f32[384,384]{1,0:T(8,128)S(1)}, f32[384,384]{1,0:T(8,128)}, u32[]{:S(2)}) copy-start(f32[384,384]{1,0:T(8,128)} %param.27) | copy-start | bytes 1769476
  701.6 66.4 %reduce-scatter.21.cloned.1.call-start = ((), (), s32[]{:S(2)}) async-start(), calls=%async_computation.21 | async-start | bytes 9437184 | tf_op jit(solution)/shard_map/reduce_scatter | solution.py:55
  753.3 223.2 %all-gather.25.cloned.1.call-start = ((), (), s32[]{:S(2)}) async-start(), calls=%async_computation.22 | async-start | bytes 14155776 | tf_op jit(solution)/shard_map/all_gather | solution.py:51
  951.6 170.6 %all-reduce.8.cloned.1.call-start = ((), (), s32[]{:S(2)}) async-start(), calls=%async_computation.25 | async-start | bytes 6488064 | tf_op jit(solution)/shard_map/psum | solution.py:362
  986.1 190.7 %all-gather.27.cloned.1.call-start = ((), (), s32[]{:S(2)}) async-start(), calls=%async_computation.24 | async-start | bytes 2654208 | tf_op jit(solution)/shard_map/all_gather | solution.py:16
  986.6 233.7 %reduce-scatter.23.cloned.1.call-start = ((), (), s32[]{:S(2)}) async-start(), calls=%async_computation.23 | async-start | bytes 4718592 | tf_op jit(solution)/shard_map/reduce_scatter | solution.py:59
  (25 other events, 187.2 us)
Sparse Core Ops, SparseCore 0:
  9.6 47.6 all-gather.10
  68.3 28.3 reduce-scatter.8
  193.4 13.3 all-gather.12
  212.8 44.5 reduce-scatter.10
  265.1 44.9 all-gather.14
  324.1 35.4 reduce-scatter.12
  389.9 26.0 all-gather.16
  427.7 44.5 reduce-scatter.14
  493.5 44.9 all-gather.18
  552.5 35.4 reduce-scatter.16
  605.1 26.0 all-gather.20
  642.9 44.5 reduce-scatter.18
  701.7 44.9 all-gather.22
  753.4 14.4 reduce-scatter.20
  951.8 23.0 all-gather.24
  986.2 135.9 all-reduce.7
  1124.1 52.5 all-gather.26
  1178.8 41.5 reduce-scatter.22
